TPU v7x, 32 devices: a whole 2x2x4 slice. The times are simulated.
32 devices in a mesh: groups: 2 (over y), sect: 16 (over z, x, core).
Axes of the slice: x: 2, y: 2, z: 4, core: 2. Of those that a mesh axis runs over, the one named last changes fastest.
Arguments:
- pattern: int32 [32], P('sect'), may hold values from 0 to 15
- thickness: float32 [32], P('sect'), may hold values from 0.5 to 1.5
- coupling: float32 [16, 2, 169, 169], replicated, may hold values from -0.0625 to 0.0625
- angles: float32 [64, 169], replicated, may hold values from -3.140625 to 3.140625
- points: int32 [2], P('groups'), parts along dimension 0, may hold values from 0 to 63
- incident: float32 [2, 2, 169, 169], P('groups'), parts along dimension 0, may hold values from -6 to 6
- monitors: int32 [16], replicated, may hold values from 0 to 168
- weights: float32 [16], replicated, may hold values from 0.05 to 0.5
Outputs:
- fields: float32 [32, 2, 2, 169, 169], P('sect', 'groups'), parts along dimension 1
- gradient: float32 [2, 32], P('groups', 'sect'), parts along dimension 0
There are 2 independent parts, one for each index of `groups`. A program takes and returns all parts, laid end to end along the dimension named above; an argument that names none is the same for every part. Nothing has to cross between parts.
All inputs are finite; a program needn't handle non-finite values.
Results may differ from a plain program's by a relative error of at most 0.0003.
Values sent between devices are 32-bit elements; how exact they have to be, the bound alone decides.
A program may use at most 128 MiB of HBM per device.

v0:
```python
import jax
import jax.numpy as jnp
from jax import lax
from jax.sharding import PartitionSpec as P

norm_scale = (1.0 + 1.0 / 22.0) ** (-0.5)
highest = lax.Precision.HIGHEST


def entering(shard, axis, combine, identity, reverse):
    length, here = (lax.axis_size(axis), lax.axis_index(axis))
    everything = jax.tree.map(lambda part: lax.all_gather(part, axis), shard)
    start = jax.tree.map(
        lambda part, zero: jnp.broadcast_to(jnp.asarray(zero, part.dtype), part.shape),
        shard,
        identity,
    )

    def hop(k, before):
        at = length - 1 - k if reverse else k
        reached = at > here if reverse else at < here
        new = combine(before, jax.tree.map(lambda part: part[at], everything))
        return jax.tree.map(lambda a, b: jnp.where(reached, a, b), new, before)

    return lax.fori_loop(0, length, hop, start)


def spread(block, axis, source):
    block = jnp.where(lax.axis_index(axis) == source, block, jnp.zeros_like(block))
    return lax.psum(block, axis)


def complex_product(left, right):
    left_real, left_imag = left
    right_real, right_imag = right
    out_real = jnp.einsum("pij,pjk->pik", left_real, right_real, precision=highest) - jnp.einsum(
        "pij,pjk->pik", left_imag, right_imag, precision=highest
    )
    out_imag = jnp.einsum("pij,pjk->pik", left_real, right_imag, precision=highest) + jnp.einsum(
        "pij,pjk->pik", left_imag, right_real, precision=highest
    )
    return (out_real, out_imag)


def combine_forward(earlier, later):
    return complex_product(later, earlier)


def combine_backward(earlier, later):
    return complex_product(earlier, later)


def apply_matrix(matrix, fields_now):
    mat_real, mat_imag = matrix
    vec_real = fields_now[:, 0]
    vec_imag = fields_now[:, 1]
    out_real = jnp.einsum("pij,pjk->pik", mat_real, vec_real, precision=highest) - jnp.einsum(
        "pij,pjk->pik", mat_imag, vec_imag, precision=highest
    )
    out_imag = jnp.einsum("pij,pjk->pik", mat_real, vec_imag, precision=highest) + jnp.einsum(
        "pij,pjk->pik", mat_imag, vec_real, precision=highest
    )
    return jnp.stack([out_real, out_imag], axis=1)


def apply_adjoint(matrix, fields_now):
    mat_real, mat_imag = matrix
    vec_real = fields_now[:, 0]
    vec_imag = fields_now[:, 1]
    out_real = jnp.einsum("pji,pjk->pik", mat_real, vec_real, precision=highest) + jnp.einsum(
        "pji,pjk->pik", mat_imag, vec_imag, precision=highest
    )
    out_imag = jnp.einsum("pji,pjk->pik", mat_real, vec_imag, precision=highest) - jnp.einsum(
        "pji,pjk->pik", mat_imag, vec_real, precision=highest
    )
    return jnp.stack([out_real, out_imag], axis=1)


def local(pattern, thickness, coupling, angles, points, incident, monitors, weights):
    harmonics = incident.shape[2]
    point_count = incident.shape[0]
    local_layers = pattern.shape[0]
    angle_rows = angles[points]
    identity_matrix = jnp.eye(harmonics, dtype=jnp.float32)
    layer_data = []
    for layer_index in range(local_layers):
        mixing_real = norm_scale * (identity_matrix + coupling[pattern[layer_index], 0])
        mixing_imag = norm_scale * coupling[pattern[layer_index], 1]
        phase = angle_rows * thickness[layer_index]
        cosine = jnp.cos(phase)[:, :, None]
        sine_part = jnp.sin(phase)[:, :, None]
        layer_real = cosine * mixing_real[None] - sine_part * mixing_imag[None]
        layer_imag = cosine * mixing_imag[None] + sine_part * mixing_real[None]
        layer_data.append(((layer_real, layer_imag), cosine, sine_part, mixing_real, mixing_imag))
    section = layer_data[0][0]
    layer_index = 1
    section = complex_product(layer_data[layer_index][0], section)
    section_real, section_imag = section
    eye_batch = identity_matrix[None]
    zero_batch = jnp.zeros(section_real.shape, jnp.float32)
    prefix = entering(
        (section_real, section_imag), "sect", combine_forward, (eye_batch, zero_batch), False
    )
    suffix = entering(
        (section_real, section_imag), "sect", combine_backward, (eye_batch, zero_batch), True
    )
    current = apply_matrix(prefix, incident)
    field_list = []
    for layer_index in range(local_layers):
        current = apply_matrix(layer_data[layer_index][0], current)
        field_list.append(current)
    fields = jnp.stack(field_list, axis=0)
    last_field = spread(current, "sect", lax.axis_size("sect") - 1)
    selector = jnp.sum(
        jnp.where(monitors[:, None] == jnp.arange(harmonics)[None, :], weights[:, None], 0.0),
        axis=0,
    )
    adjoint = apply_adjoint(
        suffix, last_field * selector[None, None, :, None] / (point_count * harmonics)
    )
    grad_list = []
    for layer_index in range(local_layers - 1, -1, -1):
        unused_matrix, cosine, sine_part, mixing_real, mixing_imag = layer_data[layer_index]
        layer_field = field_list[layer_index]
        adj_real = adjoint[:, 0]
        adj_imag = adjoint[:, 1]
        grad_list.append(
            -2.0
            * jnp.sum(
                angle_rows[:, :, None]
                * (adj_real * layer_field[:, 1] - adj_imag * layer_field[:, 0])
            )
        )
        back_real = cosine * adj_real + sine_part * adj_imag
        back_imag = cosine * adj_imag - sine_part * adj_real
        new_real = jnp.einsum(
            "ji,pjk->pik", mixing_real, back_real, precision=highest
        ) + jnp.einsum("ji,pjk->pik", mixing_imag, back_imag, precision=highest)
        new_imag = jnp.einsum(
            "ji,pjk->pik", mixing_real, back_imag, precision=highest
        ) - jnp.einsum("ji,pjk->pik", mixing_imag, back_real, precision=highest)
        adjoint = jnp.stack([new_real, new_imag], axis=1)
    gradient = jnp.stack(grad_list[::-1], axis=0)[None, :]
    return (fields, gradient)


def solution(mesh):
    in_specs = (
        P("sect"),
        P("sect"),
        P(),
        P(),
        P("groups"),
        P("groups", None, None, None),
        P(),
        P(),
    )
    out_specs = (P("sect", "groups", None, None, None), P("groups", "sect"))
    return jax.shard_map(local, mesh=mesh, in_specs=in_specs, out_specs=out_specs, check_vma=False)
```

profile of v0, /device:TPU:27, one launch (start us, length us, event | category | flops | bytes accessed | tf_op | source)
XLA Modules:
  0.0 392.3 jit_solution(12122222718518575283)
XLA Ops:
  15.8 1.9 constant_dynamic-slice_fusion.1
  21.6 40.9 %all-gather.9.cloned.1.call-done = f32[16,169,169]{2,1,0:T(8,128)} async-done(((f32[1,169,169]{2,1,0:T(8,128)}), f32[16,169,169]{2,1,0:T(8,128)}) %all-gather.9.cloned.1.call-update) | async-done | bytes 1827920 | tf_op jit(solution)/shard_map/all_gather | solution.py:12
  62.5 45.6 %all-gather.7.cloned.1.call-done = f32[16,169,169]{2,1,0:T(8,128)} async-done(((f32[1,169,169]{2,1,0:T(8,128)}), f32[16,169,169]{2,1,0:T(8,128)}) %all-gather.7.cloned.1.call-update) | async-done | bytes 1827920 | tf_op jit(solution)/shard_map/all_gather | solution.py:12
  108.1 81.1 %while.35 = (s32[]{:T(128)}, f32[1,169,169]{2,1,0:T(8,128)S(1)}, f32[1,169,169]{2,1,0:T(8,128)S(1)}, s32[]{:T(128)}, f32[16,1,169,169]{3,2,1,0:T(8,128)}, /*index=5*/f32[16,1,169,169]{3,2,1,0:T(8,128)}, s32[]{:T(128)}, s32[]{:T(128)}) while((s32[]{:T(128)}, f32[1,169,169]{2,1,0:T(8,128)S(1)}, f32[1,169,169]{2,1,0:T(8,128)S(1)}, ...), condition=%wide.region_1.2_spmd.clone, body=%wide.region_0.1_spmd.clone.sunk | while | flops 231886752 | bytes 2320444 | solution.py:25
  189.2 95.1 %while.36 = (s32[]{:T(128)}, f32[1,169,169]{1,2,0:T(8,128)S(1)}, f32[1,169,169]{1,2,0:T(8,128)S(1)}, s32[]{:T(128)}, f32[16,1,169,169]{3,2,1,0:T(8,128)}, /*inde...) while((s32[]{:T(128)}, f32[1,169,169]{1,2,0:T(8,128)S(1)}, ...), condition=%wide.region_3.4_spmd.clone, body=%wide.region_2.3_spmd.clone.sunk | while | flops 231886752 | bytes 2520487 | solution.py:25
  192.2 1.5 fusion.195
  198.1 1.5 fusion.195
  199.6 1.5 fusion.197
  204.1 1.5 fusion.195
  205.6 1.5 fusion.197
  210.0 1.5 fusion.195
  211.5 1.5 fusion.197
  216.0 1.5 fusion.195
  217.4 1.5 fusion.197
  221.9 1.5 fusion.195
  223.4 1.5 fusion.197
  227.8 1.5 fusion.195
  229.3 1.5 fusion.197
  233.8 1.5 fusion.195
  235.3 1.5 fusion.197
  239.7 1.5 fusion.195
  245.7 1.5 fusion.195
  251.6 1.5 fusion.195
  253.1 1.5 fusion.197
  257.6 1.5 fusion.195
  259.1 1.5 fusion.197
  263.5 1.5 fusion.195
  265.0 1.5 fusion.197
  269.5 1.5 fusion.195
  275.4 1.5 fusion.195
  281.4 1.5 fusion.195
  290.8 87.1 %all-reduce.2.cloned.1.call-done = f32[1,2,169,169]{3,2,1,0:T(8,128)} async-done(((f32[1,2,169,169]{3,2,1,0:T(8,128)}), f32[1,2,169,169]{3,2,1,0:T(8,128)}) %all-reduce.2.cloned.1.call-update) | async-done | bytes 228504 | tf_op jit(solution)/shard_map/psum | solution.py:30
  (188 shorter events, 156.3 us)
Async XLA Ops:
  7.2 6.0 %copy-start = (f32[64,169]{1,0:T(8,128)S(1)}, f32[64,169]{1,0:T(8,128)}, u32[]{:S(2)}) copy-start(f32[64,169]{1,0:T(8,128)} %param.15) | copy-start | bytes 129796
  7.2 55.4 %all-gather.9.cloned.1.call-start = ((), (), s32[]{:S(2)}) async-start(), calls=%async_computation.2 | async-start | bytes 3063808 | tf_op jit(solution)/shard_map/all_gather | solution.py:12
  15.7 5.5 %copy-start.2 = (f32[16]{0:T(128)S(1)}, f32[16]{0:T(128)}, u32[]{:S(2)}) copy-start(f32[16]{0:T(128)} %param.19) | copy-start | bytes 196
  15.8 5.5 %copy-start.3 = (s32[16]{0:T(128)S(1)}, s32[16]{0:T(128)}, u32[]{:S(2)}) copy-start(s32[16]{0:T(128)} %param.18) | copy-start | bytes 196
  15.8 5.5 %copy-start.1 = (f32[1,2,169,169]{3,1,2,0:T(2,128)S(1)}, f32[1,2,169,169]{3,1,2,0:T(2,128)}, u32[]{:S(2)}) copy-start(f32[1,2,169,169]{3,1,2,0:T(2,128)} %param.17) | copy-start | bytes 685468
  19.2 88.9 %all-gather.7.cloned.1.call-start = ((), (), s32[]{:S(2)}) async-start(), calls=%async_computation.1 | async-start | bytes 3063808 | tf_op jit(solution)/shard_map/all_gather | solution.py:12
  20.8 357.1 %all-reduce.2.cloned.1.call-start = ((), (), s32[]{:S(2)}) async-start(), calls=%async_computation | async-start | bytes 720896 | tf_op jit(solution)/shard_map/psum | solution.py:30
Sparse Core Ops, SparseCore 0:
  19.4 43.1 all-gather.8
  65.4 42.6 all-gather.6
  289.4 88.4 all-reduce.1
where the time goes:
time: 399 us; the launch traced here: 392 us
  matrix products  186 us (47%)
  waiting for transfers between devices  174 us (44%)
  between operations  19.9 us (5%)
  local copies, waits for them, and re-layouts  6.83 us (2%)
    psum x1, waiting for transfers between devices, spread(): return lax.psum(block, axis)  87.1 us
    all_gather x2, waiting for transfers between devices, entering(): everything = jax.tree.map(lambda part: lax.all_gather(part, axis), shard)  86.5 us
    dot_general x33, matrix products, complex_product(): jnp.einsum('pij,pjk->pik', left_imag, right_imag, precision=highest)  45.8 us
    dot_general x33, matrix products, complex_product(): jnp.einsum('pij,pjk->pik', left_imag, right_real, precision=highest)  44.2 us
    dot_general x33, matrix products, complex_product(): jnp.einsum('pij,pjk->pik', left_real, right_imag, precision=highest)  43.4 us
    dot_general x33, matrix products, complex_product(): jnp.einsum('pij,pjk->pik', left_real, right_real, precision=highest)  43.3 us
  transfers between devices with their start and end apart: 3, of which 3 were waited for; matrix products, arithmetic and copies ran while one was open for 1% of the time, Pallas kernels for 0%

commit v1 on v0

v1 whole, which is shorter than its diff:
```python
import functools
import jax
import jax.numpy as jnp
from jax import lax
from jax.experimental import pallas as pl
from jax.experimental.pallas import tpu as pltpu
from jax.sharding import PartitionSpec as P

norm_scale = (1.0 + 1.0 / 22.0) ** (-0.5)
f32 = jnp.float32
bf16 = jnp.bfloat16


def gather_kernel(count, own_ref, out_ref, send_sem, recv_sem):
    here = lax.axis_index("sect")
    barrier = pltpu.get_barrier_semaphore()

    def peer(k):
        return lax.rem(here + k, count)

    def greet(k, c):
        pl.semaphore_signal(barrier, inc=1, device_id={"sect": peer(k)}, device_id_type=pl.DeviceIdType.MESH)
        return c

    lax.fori_loop(1, count, greet, 0)
    out_ref[here] = own_ref[...]
    pl.semaphore_wait(barrier, count - 1)

    def copy(k):
        return pltpu.make_async_remote_copy(
            src_ref=own_ref,
            dst_ref=out_ref.at[here],
            send_sem=send_sem.at[k],
            recv_sem=recv_sem.at[k],
            device_id={"sect": peer(k)},
            device_id_type=pl.DeviceIdType.MESH,
        )

    def start(k, c):
        copy(k).start()
        return c

    def finish(k, c):
        copy(k).wait()
        return c

    lax.fori_loop(1, count, start, 0)
    lax.fori_loop(1, count, finish, 0)


def split(x):
    hi = x.astype(bf16)
    return hi, (x - hi.astype(f32)).astype(bf16)


def dot(a, b, transposed):
    dims = (((1,), (1 if transposed else 0,)), ((), ()))
    return lax.dot_general(a, b, dims, preferred_element_type=f32)


def dot3(a, b, transposed):
    (ah, al), (bh, bl) = (a, b)
    return dot(ah, bh, transposed) + (dot(al, bh, transposed) + dot(ah, bl, transposed))


def main_kernel(
    sections, own_layers, gathered, points, monitors, weights, coupling, angles, incident,
    fields, gradient, parts, cosines, sines, kept,
):
    here = lax.axis_index("sect")
    layers = sections * own_layers
    patterns = coupling.shape[0]
    harm = incident.shape[-1]
    mon = monitors.shape[0]

    def pattern_of(layer):
        return gathered[layer // own_layers, 0, lax.rem(layer, own_layers)].astype(jnp.int32)

    def prepare(n, c):
        real, imag = coupling[n, 0], coupling[n, 1]
        for at, value in enumerate((real, imag, real + imag)):
            hi, lo = split(value)
            parts[n, 2 * at] = hi
            parts[n, 2 * at + 1] = lo
        return c

    lax.fori_loop(0, patterns, prepare, 0)

    theta = angles[pl.ds(points[0], 1), :]

    def fill(layer, c):
        depth = gathered[layer // own_layers, 0, own_layers + lax.rem(layer, own_layers)]
        cosines[pl.ds(layer, 1), :] = theta * depth
        return c

    lax.fori_loop(0, layers, fill, 0)
    phase = cosines[...]
    sines[...] = norm_scale * jnp.sin(phase)
    cosines[...] = norm_scale * jnp.cos(phase)

    rows = lax.broadcasted_iota(jnp.int32, (mon, harm), 0)
    lanes = lax.broadcasted_iota(jnp.int32, (mon, harm), 1)
    picked = jnp.zeros((mon, harm), f32)
    scale = jnp.zeros((mon, harm), f32)
    for m in range(mon):
        picked = jnp.where((rows == m) & (lanes == monitors[m]), 1.0, picked)
        scale = jnp.where(rows == m, weights[m], scale)
    scale = scale * (1.0 / harm)

    first = here * own_layers

    def forward(layer, real, imag):
        n = pattern_of(layer)
        one = dot3(split(real), (parts[n, 0], parts[n, 1]), True)
        two = dot3(split(imag), (parts[n, 2], parts[n, 3]), True)
        three = dot3(split(real + imag), (parts[n, 4], parts[n, 5]), True)
        mixed_real = real + (one - two)
        mixed_imag = imag + (three - one - two)
        cos, sin = cosines[pl.ds(layer, 1), :], sines[pl.ds(layer, 1), :]
        return cos * mixed_real - sin * mixed_imag, cos * mixed_imag + sin * mixed_real

    def backward(layer, both):
        @pl.when((layer >= first) & (layer < first + own_layers))
        def _():
            kept[layer - first] = both

        n = pattern_of(layer)
        real, imag = both[:mon], both[mon:]
        cos, sin = cosines[pl.ds(layer, 1), :], sines[pl.ds(layer, 1), :]
        both = jnp.concatenate([cos * real - sin * imag, cos * imag + sin * real], axis=0)
        hi, lo = split(both)
        stacked = jnp.concatenate([hi, lo], axis=0)

        def times(at):
            high = dot(stacked, parts[n, at], False)
            return high[: 2 * mon] + (high[2 * mon :] + dot(hi, parts[n, at + 1], False))

        by_real, by_imag = times(0), times(2)
        return both + jnp.concatenate(
            [by_real[:mon] - by_imag[mon:], by_real[mon:] + by_imag[:mon]], axis=0
        )

    def step(i, carry):
        real, imag, both = carry
        both = backward(layers - 1 - i, both)
        real, imag = forward(i, real, imag)
        return real, imag, both

    both = jnp.concatenate([picked, jnp.zeros_like(picked)], axis=0)
    carry = (incident[0, 0].T, incident[0, 1].T, both)
    real, imag, both = lax.fori_loop(0, first, step, carry)
    own = []
    for j in range(own_layers):
        real, imag, both = step(first + j, (real, imag, both))
        own.append((real, imag))
        fields[j, 0, 0] = real.T
        fields[j, 0, 1] = imag.T
    both = lax.fori_loop(
        first + own_layers, layers, lambda i, b: backward(layers - 1 - i, b), both
    )

    start = split(both)
    by_real = dot3(start, split(incident[0, 0]), False)
    by_imag = dot3(start, split(incident[0, 1]), False)
    out_real = scale * (by_real[:mon] - by_imag[mon:])
    out_imag = scale * (by_real[mon:] + by_imag[:mon])
    target = split(jnp.concatenate([out_real, out_imag], axis=0))
    for j in range(own_layers):
        real, imag = own[j]
        by_real = dot3(target, split(real), False)
        by_imag = dot3(target, split(imag), False)
        a_real = by_real[:mon] + by_imag[mon:]
        a_imag = by_imag[:mon] - by_real[mon:]
        now = kept[j]
        total = jnp.sum(theta * (now[:mon] * a_imag + now[mon:] * a_real))
        gradient[0, j] = -2.0 * total


def local(pattern, thickness, coupling, angles, points, incident, monitors, weights):
    sections = lax.axis_size("sect")
    own_layers = pattern.shape[0]
    harm = incident.shape[-1]
    layers = sections * own_layers
    vmem = pl.BlockSpec(memory_space=pltpu.VMEM)
    smem = pl.BlockSpec(memory_space=pltpu.SMEM)
    own = jnp.concatenate([pattern.astype(f32), thickness])
    own = jnp.pad(own, (0, 128 - own.shape[0]))[None]
    gathered = pl.pallas_call(
        functools.partial(gather_kernel, sections),
        out_shape=jax.ShapeDtypeStruct((sections, 1, 128), f32),
        in_specs=[vmem],
        out_specs=vmem,
        scratch_shapes=[pltpu.SemaphoreType.DMA((sections,)), pltpu.SemaphoreType.DMA((sections,))],
        compiler_params=pltpu.CompilerParams(collective_id=0, has_side_effects=True),
    )(own)
    return pl.pallas_call(
        functools.partial(main_kernel, sections, own_layers),
        out_shape=(
            jax.ShapeDtypeStruct((own_layers, 1, 2, harm, harm), f32),
            jax.ShapeDtypeStruct((1, own_layers), f32),
        ),
        in_specs=[smem, smem, smem, smem, vmem, vmem, vmem],
        out_specs=(vmem, smem),
        scratch_shapes=[
            pltpu.VMEM((coupling.shape[0], 6, harm, harm), bf16),
            pltpu.VMEM((layers, harm), f32),
            pltpu.VMEM((layers, harm), f32),
            pltpu.VMEM((own_layers, 2 * monitors.shape[0], harm), f32),
        ],
        compiler_params=pltpu.CompilerParams(vmem_limit_bytes=40 * 2**20),
    )(gathered, points, monitors, weights, coupling, angles, incident)


def solution(mesh):
    in_specs = (
        P("sect"), P("sect"), P(), P(), P("groups"),
        P("groups", None, None, None), P(), P(),
    )
    out_specs = (P("sect", "groups", None, None, None), P("groups", "sect"))
    return jax.shard_map(local, mesh=mesh, in_specs=in_specs, out_specs=out_specs, check_vma=False)
```

time: 399 us -> 37.5 us (0.09); the launches traced: 392 us -> 37.3 us
  matrix products: 186 us -> 0 us
  waiting for transfers between devices: 174 us -> 0 us
  Pallas kernels: 0 us -> 28.4 us
  between operations: 19.9 us -> 1.37 us
    dot_general x152 -> x0, matrix products: 186 us -> none  [the longest x33 45.8 us: complex_product(): jnp.einsum('pij,pjk->pik', left_imag, right_imag, precision=highest)]
    psum x1 -> x0, waiting for transfers between devices: 87.1 us -> none  [spread(): return lax.psum(block, axis)]
    all_gather x2 -> x0, waiting for transfers between devices: 86.5 us -> none  [entering(): everything = jax.tree.map(lambda part: lax.all_gather(part, axis), shard)]
    pallas_call x0 -> x2, Pallas kernels: none -> 28.4 us  [the longest x1 20.6 us: local(): pl.pallas_call(functools.partial(main_kernel, sections, own_layers), out_...]
  transfers between devices with their start and end apart: 3 -> 0, of which waited for: 3 -> 0; matrix products, arithmetic and copies ran while one was open for 1% -> 0% of each run, Pallas kernels for 0% -> 0%
where the time goes in v1:
time: 37.5 us; the launch traced here: 37.3 us
  Pallas kernels  28.4 us (76%)
  local copies, waits for them, and re-layouts  5.69 us (15%)
  other arithmetic  1.9 us (5%)
  between operations  1.37 us (4%)
    pallas_call x1, Pallas kernels, local(): pl.pallas_call(functools.partial(main_kernel, sections, own_layers), out_...  20.6 us
    pallas_call x1, Pallas kernels, local(): pl.pallas_call(functools.partial(gather_kernel, sections), out_shape=jax....  7.82 us
    unnamed x10, local copies, waits for them, and re-layouts  4.3 us
    pallas_call x1, local copies, waits for them, and re-layouts, local(): pl.pallas_call(functools.partial(main_kernel, sections, own_layers), out_...  1.38 us
    broadcast_in_dim x1, other arithmetic, local(): own = jnp.pad(own, (0, 128 - own.shape[0]))[None]  1.24 us

profile of v1, /device:TPU:27, one launch (start us, length us, event | category | flops | bytes accessed | tf_op | source)
XLA Modules:
  0.0 37.3 jit_solution(5823724285018213989)
XLA Ops:
  1.3 0.7 %convert_element_type.5 = f32[2]{0:T(128)S(1)} convert(s32[2]{0:T(128)} %param.8) | non-fusion elementwise | flops 2 | bytes 16 | tf_op jit(solution)/shard_map/convert_element_type | solution.py:186
  1.9 1.2 %fusion.1.own_ref = f32[1,128]{1,0:T(1,128)} fusion(f32[2]{0:T(128)} %param.9, f32[2]{0:T(128)S(1)} %convert_element_type.5), kind=kLoop, calls=%fused_computation.3 | loop fusion | flops 512 | bytes 528 | tf_op jit(solution)/shard_map/broadcast_in_dim | solution.py:187
  3.2 7.8 %shard_map.95.gathered = f32[16,1,128]{2,1,0:T(1,128)} custom-call(f32[1,128]{1,0:T(1,128)} %fusion.1.own_ref), custom_call_target="tpu_custom_call" | custom-call | tf_op jit(solution)/shard_map/pallas_call | solution.py:188
  11.0 1.0 %copy.11.incident = f32[1,2,169,169]{3,2,1,0:T(8,128)S(1)} copy(f32[1,2,169,169]{3,1,2,0:T(2,128)} %param.13) | data formatting | bytes 456976 | tf_op args[5]
  12.0 0.0 copy-start
  12.0 0.0 copy-start.1
  12.0 0.0 copy-start.2
  12.0 0.0 copy-start.3
  12.1 3.3 %copy.10.coupling = f32[16,2,169,169]{3,2,1,0:T(8,128)S(1)} copy(f32[16,2,169,169]{3,1,2,0:T(2,128)} %param.10) | data formatting | bytes 7311616 | tf_op args[2]
  15.3 0.0 copy-done
  15.4 0.0 copy-done.1
  15.4 0.0 copy-done.2
  15.4 0.0 copy-done.3
  15.4 20.6 %shard_map.96 = (f32[2,1,2,169,169]{4,3,2,1,0:T(8,128)S(1)}, f32[1,2]{1,0:T(1,128)}) custom-call(f32[16,1,128]{2,1,0:T(1,128)S(1)} %copy-done.1, s32[1]{0:T(128)S(6)} %copy.13.points, s32[16]{0:T(128)S(1)} %copy-done.2, f32[16]{0:T(128)S(1)} %copy-done.3, f32[16,2,169,169]{3,2,1,0:T(8,128)S(1)} %copy.10.coupling, f32[64,169]{1,0:T(8,128)S(1)} %copy-done, ...), custom_call_target="tpu_custom_call" | custom-call | tf_op jit(solution)/shard_map/pallas_call | solution.py:196
  35.9 1.4 %copy.12 = f32[2,1,2,169,169]{4,2,3,1,0:T(2,128)} copy(f32[2,1,2,169,169]{4,3,2,1,0:T(8,128)S(1)} %get-tuple-element.2) | data formatting | bytes 913952 | tf_op jit(solution)/shard_map/pallas_call | solution.py:196
Async XLA Ops:
  12.0 3.3 %copy-start = (f32[64,169]{1,0:T(8,128)S(1)}, f32[64,169]{1,0:T(8,128)}, u32[]{:S(2)}) copy-start(f32[64,169]{1,0:T(8,128)} %angles.1) | copy-start | bytes 129796
  12.0 3.3 %copy-start.1 = (f32[16,1,128]{2,1,0:T(1,128)S(1)}, f32[16,1,128]{2,1,0:T(1,128)}, u32[]{:S(2)}) copy-start(f32[16,1,128]{2,1,0:T(1,128)} %shard_map.95.gathered) | copy-start | bytes 24580
  12.0 3.3 %copy-start.2 = (s32[16]{0:T(128)S(1)}, s32[16]{0:T(128)}, u32[]{:S(2)}) copy-start(s32[16]{0:T(128)} %monitors.1) | copy-start | bytes 196
  12.0 3.3 %copy-start.3 = (f32[16]{0:T(128)S(1)}, f32[16]{0:T(128)}, u32[]{:S(2)}) copy-start(f32[16]{0:T(128)} %weights.1) | copy-start | bytes 196

commit v2 on v1

v2 whole, which is shorter than its diff:
```python
import functools
import jax
import jax.numpy as jnp
from jax import lax
from jax.experimental import pallas as pl
from jax.experimental.pallas import tpu as pltpu
from jax.sharding import PartitionSpec as P

norm_scale = (1.0 + 1.0 / 22.0) ** (-0.5)
f32 = jnp.float32
bf16 = jnp.bfloat16


def split(x):
    hi = x.astype(bf16)
    return hi, (x - hi.astype(f32)).astype(bf16)


def dot(a, b, transposed):
    dims = (((1,), (1 if transposed else 0,)), ((), ()))
    return lax.dot_general(a, b, dims, preferred_element_type=f32)


def dot3(a, b, transposed):
    (ah, al), (bh, bl) = (a, b)
    return dot(ah, bh, transposed) + (dot(al, bh, transposed) + dot(ah, bl, transposed))


MESH = pl.DeviceIdType.MESH
cores = 2


def main_kernel(
    sections, own_layers, pattern, thickness, points, monitors, weights, coupling, angles, incident,
    fields, gradient, table, parts, start_fields, cosines, sines, kept, angle_rows, inc, whole, leaving,
    ids, depths, ids_smem, depths_smem,
    load_sem, more_sem, small_sem, send_sem, recv_sem, swap_send, swap_recv,
):
    here = lax.axis_index("sect")
    layers = sections * own_layers
    patterns = coupling.shape[0]
    harm = incident.shape[-1]
    mon = monitors.shape[0]
    share = leaving.shape[2]
    core = lax.rem(here, cores)
    chip_first = (here - core) * own_layers
    first = here * own_layers
    barrier = pltpu.get_barrier_semaphore()

    def peer(k):
        return lax.rem(here + k, sections)

    def greet(k, c):
        pl.semaphore_signal(barrier, inc=1, device_id={"sect": peer(k)}, device_id_type=MESH)
        return c

    lax.fori_loop(1, sections, greet, 0)

    def load(n):
        return pltpu.make_async_copy(coupling.at[n], table.at[n], load_sem.at[n])

    def load_start(n, c):
        load(n).start()
        return c

    more = (
        pltpu.make_async_copy(incident, inc, more_sem.at[0]),
        pltpu.make_async_copy(angles, angle_rows, more_sem.at[1]),
    )
    lax.fori_loop(0, patterns, load_start, 0)
    for copy in more:
        copy.start()

    lane = lax.broadcasted_iota(jnp.int32, (1, 128), 1)
    id_row = jnp.zeros((1, 128), jnp.int32)
    depth_row = jnp.zeros((1, 128), f32)
    for j in range(own_layers):
        id_row = jnp.where(lane == j, pattern[j], id_row)
        depth_row = jnp.where(lane == j, thickness[j], depth_row)
    ids[here] = id_row
    depths[here] = depth_row
    pl.semaphore_wait(barrier, sections - 1)

    def sends(k):
        return tuple(
            pltpu.make_async_remote_copy(
                src_ref=rows.at[here],
                dst_ref=rows.at[here],
                send_sem=send_sem.at[at, k],
                recv_sem=recv_sem.at[at, k],
                device_id={"sect": peer(k)},
                device_id_type=MESH,
            )
            for at, rows in enumerate((ids, depths))
        )

    def send_start(k, c):
        for copy in sends(k):
            copy.start()
        return c

    def send_finish(k, c):
        for copy in sends(k):
            copy.wait()
        return c

    lax.fori_loop(1, sections, send_start, 0)

    def prepare(n, c):
        load(n).wait()
        real, imag = table[n, :, 0, :], table[n, :, 1, :]
        for at, value in enumerate((real, imag, real + imag)):
            hi, lo = split(value)
            parts[n, 2 * at] = hi
            parts[n, 2 * at + 1] = lo
        return c

    lax.fori_loop(0, patterns, prepare, 0)
    for copy in more:
        copy.wait()
    for c in range(2):
        start_fields[c] = jnp.zeros_like(start_fields[c])
        start_fields[c, :harm, :] = inc[0, :, c, :].T
    theta = angle_rows[pl.ds(points[0], 1), :]

    rows = lax.broadcasted_iota(jnp.int32, (mon, harm), 0)
    lanes = lax.broadcasted_iota(jnp.int32, (mon, harm), 1)
    picked = jnp.zeros((mon, harm), f32)
    scale = jnp.zeros((mon, harm), f32)
    for m in range(mon):
        picked = jnp.where((rows == m) & (lanes == monitors[m]), 1.0, picked)
        scale = jnp.where(rows == m, weights[m], scale)
    scale = scale * (1.0 / harm)

    lax.fori_loop(1, sections, send_finish, 0)
    small = (
        pltpu.make_async_copy(ids, ids_smem, small_sem.at[0]),
        pltpu.make_async_copy(depths, depths_smem, small_sem.at[1]),
    )
    for copy in small:
        copy.start()
    for copy in small:
        copy.wait()

    def pattern_of(layer):
        return ids_smem[layer // own_layers, 0, lax.rem(layer, own_layers)]

    def fill(layer, c):
        depth = depths_smem[layer // own_layers, 0, lax.rem(layer, own_layers)]
        cosines[pl.ds(layer, 1), :] = theta * depth
        return c

    lax.fori_loop(0, layers, fill, 0)
    phase = cosines[...]
    sines[...] = norm_scale * jnp.sin(phase)
    cosines[...] = norm_scale * jnp.cos(phase)

    def forward(layer, real, imag):
        n = pattern_of(layer)
        one = dot3(split(real), (parts[n, 0], parts[n, 1]), True)
        two = dot3(split(imag), (parts[n, 2], parts[n, 3]), True)
        three = dot3(split(real + imag), (parts[n, 4], parts[n, 5]), True)
        mixed_real = real + (one - two)
        mixed_imag = imag + (three - one - two)
        cos, sin = cosines[pl.ds(layer, 1), :], sines[pl.ds(layer, 1), :]
        return cos * mixed_real - sin * mixed_imag, cos * mixed_imag + sin * mixed_real

    def backward(layer, both):
        @pl.when((layer >= first) & (layer < first + own_layers))
        def _():
            kept[layer - first] = both

        n = pattern_of(layer)
        real, imag = both[:mon], both[mon:]
        cos, sin = cosines[pl.ds(layer, 1), :], sines[pl.ds(layer, 1), :]
        both = jnp.concatenate([cos * real - sin * imag, cos * imag + sin * real], axis=0)
        hi, lo = split(both)
        stacked = jnp.concatenate([hi, lo], axis=0)

        def times(at):
            high = dot(stacked, parts[n, at], False)
            return high[: 2 * mon] + (high[2 * mon :] + dot(hi, parts[n, at + 1], False))

        by_real, by_imag = times(0), times(2)
        return both + jnp.concatenate(
            [by_real[:mon] - by_imag[mon:], by_real[mon:] + by_imag[:mon]], axis=0
        )

    def step(i, carry):
        real, imag, both = carry
        both = backward(layers - 1 - i, both)
        real, imag = forward(i, real, imag)
        return real, imag, both

    own_rows = pl.ds(pl.multiple_of(core * share, 8), share)

    def swap(j):
        return pltpu.make_async_remote_copy(
            src_ref=leaving.at[j],
            dst_ref=whole.at[j, :, own_rows, :],
            send_sem=swap_send.at[j],
            recv_sem=swap_recv.at[j],
            device_id={"sect": here + 1 - 2 * core},
            device_id_type=MESH,
        )

    both = jnp.concatenate([picked, jnp.zeros_like(picked)], axis=0)
    carry = (start_fields[0, own_rows, :], start_fields[1, own_rows, :], both)
    real, imag, both = lax.fori_loop(0, chip_first, step, carry)
    for owner in range(cores):
        for j in range(own_layers):
            i = chip_first + owner * own_layers + j
            real, imag, both = step(i, (real, imag, both))

            @pl.when(core == owner)
            def _():
                whole[j, 0, own_rows, :] = real
                whole[j, 1, own_rows, :] = imag

            @pl.when(core != owner)
            def _():
                leaving[j, 0] = real
                leaving[j, 1] = imag
                swap(j).start()

    both = lax.fori_loop(
        chip_first + cores * own_layers, layers, lambda i, b: backward(layers - 1 - i, b), both
    )

    start = split(both)
    by_real = dot3(start, split(inc[0, :, 0, :]), False)
    by_imag = dot3(start, split(inc[0, :, 1, :]), False)
    out_real = scale * (by_real[:mon] - by_imag[mon:])
    out_imag = scale * (by_real[mon:] + by_imag[:mon])
    target = split(jnp.concatenate([out_real, out_imag], axis=0))
    for j in range(own_layers):
        swap(j).wait()
        real, imag = whole[j, 0, :harm, :], whole[j, 1, :harm, :]
        fields[j, 0, :, 0, :] = real.T
        fields[j, 0, :, 1, :] = imag.T
        by_real = dot3(target, split(real), False)
        by_imag = dot3(target, split(imag), False)
        a_real = by_real[:mon] + by_imag[mon:]
        a_imag = by_imag[:mon] - by_real[mon:]
        now = kept[j]
        total = jnp.sum(theta * (now[:mon] * a_imag + now[mon:] * a_real))
        gradient[0, j] = -2.0 * total


def local(pattern, thickness, coupling, angles, points, incident, monitors, weights):
    sections = lax.axis_size("sect")
    own_layers = pattern.shape[0]
    patterns = coupling.shape[0]
    harm = incident.shape[-1]
    layers = sections * own_layers
    share = -(-harm // (8 * cores)) * 8
    vmem = pl.BlockSpec(memory_space=pltpu.VMEM)
    smem = pl.BlockSpec(memory_space=pltpu.SMEM)
    hbm = pl.BlockSpec(memory_space=pltpu.HBM)
    dma = pltpu.SemaphoreType.DMA
    fields, gradient = pl.pallas_call(
        functools.partial(main_kernel, sections, own_layers),
        out_shape=(
            jax.ShapeDtypeStruct((own_layers, 1, harm, 2, harm), f32),
            jax.ShapeDtypeStruct((1, own_layers), f32),
        ),
        in_specs=[smem] * 5 + [hbm] * 3,
        out_specs=(vmem, smem),
        scratch_shapes=[
            pltpu.VMEM((patterns, harm, 2, harm), f32),
            pltpu.VMEM((patterns, 6, harm, harm), bf16),
            pltpu.VMEM((2, cores * share, harm), f32),
            pltpu.VMEM((layers, harm), f32),
            pltpu.VMEM((layers, harm), f32),
            pltpu.VMEM((own_layers, 2 * monitors.shape[0], harm), f32),
            pltpu.VMEM(angles.shape, f32),
            pltpu.VMEM((1, harm, 2, harm), f32),
            pltpu.VMEM((own_layers, 2, cores * share, harm), f32),
            pltpu.VMEM((own_layers, 2, share, harm), f32),
            pltpu.VMEM((sections, 1, 128), jnp.int32),
            pltpu.VMEM((sections, 1, 128), f32),
            pltpu.SMEM((sections, 1, 128), jnp.int32),
            pltpu.SMEM((sections, 1, 128), f32),
            dma((patterns,)),
            dma((2,)),
            dma((2,)),
            dma((2, sections)),
            dma((2, sections)),
            dma((own_layers,)),
            dma((own_layers,)),
        ],
        compiler_params=pltpu.CompilerParams(
            collective_id=0, has_side_effects=True, vmem_limit_bytes=63 * 2**20
        ),
    )(
        pattern, thickness, points, monitors, weights,
        coupling.transpose(0, 2, 1, 3), angles, incident.transpose(0, 2, 1, 3),
    )
    return fields.transpose(0, 1, 3, 2, 4), gradient


def solution(mesh):
    in_specs = (
        P("sect"), P("sect"), P(), P(), P("groups"),
        P("groups", None, None, None), P(), P(),
    )
    out_specs = (P("sect", "groups", None, None, None), P("groups", "sect"))
    return jax.shard_map(local, mesh=mesh, in_specs=in_specs, out_specs=out_specs, check_vma=False)
```

time: 37.5 us -> 54.3 us (1.45)
  Pallas kernels: 28.4 us -> 49.5 us
  local copies, waits for them, and re-layouts: 5.69 us -> 3.33 us
  other arithmetic: 1.9 us -> 0 us
    pallas_call x1, Pallas kernels: 20.6 us -> 49.5 us  [local(): pl.pallas_call(functools.partial(main_kernel, sections, own_layers), out_...]
    pallas_call x1 -> x0, Pallas kernels: 7.82 us -> none  [local(): pl.pallas_call(functools.partial(gather_kernel, sections), out_shape=jax....]
    pallas_call x1 -> x0, local copies, waits for them, and re-layouts: 1.38 us -> none  [local(): pl.pallas_call(functools.partial(main_kernel, sections, own_layers), out_...]
    broadcast_in_dim x1 -> x0, other arithmetic: 1.24 us -> none  [local(): own = jnp.pad(own, (0, 128 - own.shape[0]))[None]]
    unnamed x10 -> x2, local copies, waits for them, and re-layouts: 4.3 us -> 3.33 us
    convert_element_type x1 -> x0, other arithmetic: 0.66 us -> none  [local(): own = jnp.concatenate([pattern.astype(f32), thickness])]
where the time goes in v2:
time: 54.3 us; the launch traced here: 54.1 us
  Pallas kernels  49.5 us (91%)
  local copies, waits for them, and re-layouts  3.33 us (6%)
  between operations  1.29 us (2%)
    pallas_call x1, Pallas kernels, local(): pl.pallas_call(functools.partial(main_kernel, sections, own_layers), out_...  49.5 us
    unnamed x2, local copies, waits for them, and re-layouts  3.33 us

profile of v2, /device:TPU:27, one launch (start us, length us, event | category | flops | bytes accessed | tf_op | source)
XLA Modules:
  0.0 54.1 jit_solution(16890871354555947892)
XLA Ops:
  1.3 49.5 %shard_map.95 = (f32[2,1,169,2,169]{4,3,2,1,0:T(2,128)}, f32[1,2]{1,0:T(1,128)}) custom-call(s32[2]{0:T(128)} %pattern.1, f32[2]{0:T(128)} %thickness.1, s32[1]{0:T(128)S(6)} %copy.12.points, s32[16]{0:T(128)} %monitors.1, f32[16]{0:T(128)} %weights.1, f32[16,169,2,169]{3,2,1,0:T(2,128)} %bitcast.3, f32[64,169]{1,0:T(8,128)} %angles.1, ...), custom_call_target="tpu_custom_call" | custom-call | tf_op jit(solution)/shard_map/pallas_call | solution.py:261
  50.8 2.2 %copy.13 = f32[2,1,2,169,169]{4,2,3,1,0:T(2,128)} copy(f32[2,1,2,169,169]{4,2,3,1,0:T(2,128)} %bitcast.4) | data formatting | bytes 913952
  53.0 1.1 %copy.14 = f32[1,2]{1,0:T(1,128)} copy(f32[1,2]{1,0:T(1,128)} %get-tuple-element.9) | data formatting | bytes 16

commit v3 on v1

--- a/solution.py
+++ b/solution.py
@@ -77,7 +77,7 @@
         return gathered[layer // own_layers, 0, lax.rem(layer, own_layers)].astype(jnp.int32)
 
     def prepare(n, c):
-        real, imag = coupling[n, 0], coupling[n, 1]
+        real, imag = coupling[n, :, 0, :], coupling[n, :, 1, :]
         for at, value in enumerate((real, imag, real + imag)):
             hi, lo = split(value)
             parts[n, 2 * at] = hi
@@ -147,21 +147,21 @@
         return real, imag, both
 
     both = jnp.concatenate([picked, jnp.zeros_like(picked)], axis=0)
-    carry = (incident[0, 0].T, incident[0, 1].T, both)
+    carry = (incident[0, :, 0, :].T, incident[0, :, 1, :].T, both)
     real, imag, both = lax.fori_loop(0, first, step, carry)
     own = []
     for j in range(own_layers):
         real, imag, both = step(first + j, (real, imag, both))
         own.append((real, imag))
-        fields[j, 0, 0] = real.T
-        fields[j, 0, 1] = imag.T
+        fields[j, 0, :, 0, :] = real.T
+        fields[j, 0, :, 1, :] = imag.T
     both = lax.fori_loop(
         first + own_layers, layers, lambda i, b: backward(layers - 1 - i, b), both
     )
 
     start = split(both)
-    by_real = dot3(start, split(incident[0, 0]), False)
-    by_imag = dot3(start, split(incident[0, 1]), False)
+    by_real = dot3(start, split(incident[0, :, 0, :]), False)
+    by_imag = dot3(start, split(incident[0, :, 1, :]), False)
     out_real = scale * (by_real[:mon] - by_imag[mon:])
     out_imag = scale * (by_real[mon:] + by_imag[:mon])
     target = split(jnp.concatenate([out_real, out_imag], axis=0))
@@ -193,10 +193,10 @@
         scratch_shapes=[pltpu.SemaphoreType.DMA((sections,)), pltpu.SemaphoreType.DMA((sections,))],
         compiler_params=pltpu.CompilerParams(collective_id=0, has_side_effects=True),
     )(own)
-    return pl.pallas_call(
+    fields, gradient = pl.pallas_call(
         functools.partial(main_kernel, sections, own_layers),
         out_shape=(
-            jax.ShapeDtypeStruct((own_layers, 1, 2, harm, harm), f32),
+            jax.ShapeDtypeStruct((own_layers, 1, harm, 2, harm), f32),
             jax.ShapeDtypeStruct((1, own_layers), f32),
         ),
         in_specs=[smem, smem, smem, smem, vmem, vmem, vmem],
@@ -208,7 +208,11 @@
             pltpu.VMEM((own_layers, 2 * monitors.shape[0], harm), f32),
         ],
         compiler_params=pltpu.CompilerParams(vmem_limit_bytes=40 * 2**20),
-    )(gathered, points, monitors, weights, coupling, angles, incident)
+    )(
+        gathered, points, monitors, weights,
+        coupling.transpose(0, 2, 1, 3), angles, incident.transpose(0, 2, 1, 3),
+    )
+    return fields.transpose(0, 1, 3, 2, 4), gradient
 
 
 def solution(mesh):

time: 37.5 us -> 64.3 us (1.71)
  Pallas kernels: 28.4 us -> 54.4 us
  local copies, waits for them, and re-layouts: 5.69 us -> 6.39 us
    pallas_call x1, Pallas kernels: 20.6 us -> 46.6 us  [local(): pl.pallas_call(functools.partial(main_kernel, sections, own_layers), out_...]
    unnamed x10 -> x12, local copies, waits for them, and re-layouts: 4.3 us -> 6.39 us
    pallas_call x1 -> x0, local copies, waits for them, and re-layouts: 1.38 us -> none  [local(): pl.pallas_call(functools.partial(main_kernel, sections, own_layers), out_...]
where the time goes in v3:
time: 64.3 us; the launch traced here: 64 us
  Pallas kernels  54.4 us (85%)
  local copies, waits for them, and re-layouts  6.39 us (10%)
  other arithmetic  1.9 us (3%)
  between operations  1.3 us (2%)
    pallas_call x1, Pallas kernels, local(): pl.pallas_call(functools.partial(main_kernel, sections, own_layers), out_...  46.6 us
    pallas_call x1, Pallas kernels, local(): pl.pallas_call(functools.partial(gather_kernel, sections), out_shape=jax....  7.83 us
    unnamed x12, local copies, waits for them, and re-layouts  6.39 us

profile of v3, /device:TPU:27, one launch (start us, length us, event | category | flops | bytes accessed | tf_op | source)
XLA Modules:
  0.0 64.0 jit_solution(6664037157326835077)
XLA Ops:
  1.3 0.7 %convert_element_type.5 = f32[2]{0:T(128)S(1)} convert(s32[2]{0:T(128)} %param.8) | non-fusion elementwise | flops 2 | bytes 16 | tf_op jit(solution)/shard_map/convert_element_type | solution.py:186
  1.9 1.2 %fusion.1.own_ref = f32[1,128]{1,0:T(1,128)} fusion(f32[2]{0:T(128)} %param.9, f32[2]{0:T(128)S(1)} %convert_element_type.5), kind=kLoop, calls=%fused_computation.3 | loop fusion | flops 512 | bytes 528 | tf_op jit(solution)/shard_map/broadcast_in_dim | solution.py:187
  3.2 7.8 %shard_map.95.gathered = f32[16,1,128]{2,1,0:T(1,128)} custom-call(f32[1,128]{1,0:T(1,128)} %fusion.1.own_ref), custom_call_target="tpu_custom_call" | custom-call | tf_op jit(solution)/shard_map/pallas_call | solution.py:188
  11.0 0.0 copy-start
  11.0 2.6 %copy-done = f32[16,2,169,169]{3,1,2,0:T(2,128)S(1)} copy-done((f32[16,2,169,169]{3,1,2,0:T(2,128)S(1)}, f32[16,2,169,169]{3,1,2,0:T(2,128)}, u32[]{:S(2)}) %copy-start) | copy-done | bytes 3655832
  13.6 0.0 copy-start.1
  13.6 1.0 %copy-done.1 = f32[1,2,169,169]{3,1,2,0:T(2,128)S(1)} copy-done((f32[1,2,169,169]{3,1,2,0:T(2,128)S(1)}, f32[1,2,169,169]{3,1,2,0:T(2,128)}, u32[]{:S(2)}) %copy-start.1) | copy-done | bytes 228512
  14.6 0.0 copy-start.2
  14.6 0.8 %copy-done.2 = f32[64,169]{1,0:T(8,128)S(1)} copy-done((f32[64,169]{1,0:T(8,128)S(1)}, f32[64,169]{1,0:T(8,128)}, u32[]{:S(2)}) %copy-start.2) | copy-done | bytes 43288
  15.4 0.0 copy-start.3
  15.4 0.7 %copy-done.3 = f32[16,1,128]{2,1,0:T(1,128)S(1)} copy-done((f32[16,1,128]{2,1,0:T(1,128)S(1)}, f32[16,1,128]{2,1,0:T(1,128)}, u32[]{:S(2)}) %copy-start.3) | copy-done | bytes 8216
  16.1 0.0 copy-start.4
  16.1 0.7 %copy-done.4 = s32[16]{0:T(128)S(1)} copy-done((s32[16]{0:T(128)S(1)}, s32[16]{0:T(128)}, u32[]{:S(2)}) %copy-start.4) | copy-done | bytes 88
  16.8 0.0 copy-start.5
  16.8 0.7 %copy-done.5 = f32[16]{0:T(128)S(1)} copy-done((f32[16]{0:T(128)S(1)}, f32[16]{0:T(128)}, u32[]{:S(2)}) %copy-start.5) | copy-done | bytes 88
  17.4 46.6 %shard_map.96 = (f32[2,1,169,2,169]{4,3,2,1,0:T(2,128)}, f32[1,2]{1,0:T(1,128)}) custom-call(f32[16,1,128]{2,1,0:T(1,128)S(1)} %copy-done.3, s32[1]{0:T(128)S(6)} %copy.10.points, s32[16]{0:T(128)S(1)} %copy-done.4, f32[16]{0:T(128)S(1)} %copy-done.5, f32[16,169,2,169]{3,2,1,0:T(2,128)S(1)} %bitcast.5, f32[64,169]{1,0:T(8,128)S(1)} %copy-done.2, ...), custom_call_target="tpu_custom_call" | custom-call | tf_op jit(solution)/shard_map/pallas_call | solution.py:196
Async XLA Ops:
  11.0 2.6 %copy-start = (f32[16,2,169,169]{3,1,2,0:T(2,128)S(1)}, f32[16,2,169,169]{3,1,2,0:T(2,128)}, u32[]{:S(2)}) copy-start(f32[16,2,169,169]{3,1,2,0:T(2,128)} %param.10) | copy-start | bytes 10967428
  13.6 1.0 %copy-start.1 = (f32[1,2,169,169]{3,1,2,0:T(2,128)S(1)}, f32[1,2,169,169]{3,1,2,0:T(2,128)}, u32[]{:S(2)}) copy-start(f32[1,2,169,169]{3,1,2,0:T(2,128)} %param.13) | copy-start | bytes 685468
  14.6 0.8 %copy-start.2 = (f32[64,169]{1,0:T(8,128)S(1)}, f32[64,169]{1,0:T(8,128)}, u32[]{:S(2)}) copy-start(f32[64,169]{1,0:T(8,128)} %angles.1) | copy-start | bytes 129796
  15.4 0.7 %copy-start.3 = (f32[16,1,128]{2,1,0:T(1,128)S(1)}, f32[16,1,128]{2,1,0:T(1,128)}, u32[]{:S(2)}) copy-start(f32[16,1,128]{2,1,0:T(1,128)} %shard_map.95.gathered) | copy-start | bytes 24580
  16.1 0.7 %copy-start.4 = (s32[16]{0:T(128)S(1)}, s32[16]{0:T(128)}, u32[]{:S(2)}) copy-start(s32[16]{0:T(128)} %monitors.1) | copy-start | bytes 196
  16.8 0.7 %copy-start.5 = (f32[16]{0:T(128)S(1)}, f32[16]{0:T(128)}, u32[]{:S(2)}) copy-start(f32[16]{0:T(128)} %weights.1) | copy-start | bytes 196
